TPU v7x, 32 devices: a whole 2x2x4 slice. The times are simulated.
32 devices in a mesh: seq: 2 (over x), fsdp: 16 (over z, y, core).
Axes of the slice: x: 2, y: 2, z: 4, core: 2. Of those that a mesh axis runs over, the one named last changes fastest.
Arguments:
- frames_in: float32 [16, 256, 768], P('fsdp', 'seq'), may hold values from -6 to 6
- cotangent: float32 [16, 256, 768], P('fsdp', 'seq'), may hold values from -6 to 6
- first_gain: bfloat16 [1, 768], P(None, 'fsdp'), may hold values from 0.099609375 to 1.8984375
- first_bias: bfloat16 [1, 768], P(None, 'fsdp'), may hold values from -3 to 3
- query_weight: bfloat16 [1, 768, 768], P(None, 'fsdp'), may hold values from -0.21875 to 0.21875
- query_bias: bfloat16 [1, 768], P(None, 'fsdp'), may hold values from -3 to 3
- key_weight: bfloat16 [1, 768, 768], P(None, 'fsdp'), may hold values from -0.21875 to 0.21875
- value_weight: bfloat16 [1, 768, 768], P(None, 'fsdp'), may hold values from -0.21875 to 0.21875
- value_bias: bfloat16 [1, 768], P(None, 'fsdp'), may hold values from -3 to 3
- out_weight: bfloat16 [1, 768, 768], P(None, 'fsdp'), may hold values from -3.5 to 3.5
- out_bias: bfloat16 [1, 768], P(None, 'fsdp'), may hold values from -3 to 3
- second_gain: bfloat16 [1, 768], P(None, 'fsdp'), may hold values from 0.099609375 to 1.8984375
- second_bias: bfloat16 [1, 768], P(None, 'fsdp'), may hold values from -3 to 3
- up_weight: bfloat16 [1, 768, 3072], P(None, 'fsdp'), may hold values from -0.21875 to 0.21875
- up_bias: bfloat16 [1, 3072], P(None, 'fsdp'), may hold values from -3 to 3
- down_weight: bfloat16 [1, 3072, 768], P(None, 'fsdp'), may hold values from -0.109375 to 0.109375
- down_bias: bfloat16 [1, 768], P(None, 'fsdp'), may hold values from -3 to 3
Outputs:
- outputs: float32 [16, 256, 768], P('fsdp', 'seq')
- input_gradient: float32 [16, 256, 768], P('fsdp', 'seq')
- first_gain_gradient: float32 [1, 768], P(None, 'fsdp')
- first_bias_gradient: float32 [1, 768], P(None, 'fsdp')
- query_weight_gradient: float32 [1, 768, 768], P(None, 'fsdp')
- query_bias_gradient: float32 [1, 768], P(None, 'fsdp')
- key_weight_gradient: float32 [1, 768, 768], P(None, 'fsdp')
- value_weight_gradient: float32 [1, 768, 768], P(None, 'fsdp')
- value_bias_gradient: float32 [1, 768], P(None, 'fsdp')
- out_weight_gradient: float32 [1, 768, 768], P(None, 'fsdp')
- out_bias_gradient: float32 [1, 768], P(None, 'fsdp')
- second_gain_gradient: float32 [1, 768], P(None, 'fsdp')
- second_bias_gradient: float32 [1, 768], P(None, 'fsdp')
- up_weight_gradient: float32 [1, 768, 3072], P(None, 'fsdp')
- up_bias_gradient: float32 [1, 3072], P(None, 'fsdp')
- down_weight_gradient: float32 [1, 3072, 768], P(None, 'fsdp')
- down_bias_gradient: float32 [1, 768], P(None, 'fsdp')
All inputs are finite; a program needn't handle non-finite values.
Results may differ from a plain program's by a relative error of at most 0.012.
The roundings to bfloat16 on the way count: a program that leaves them out, or rounds other values in their place, can miss the bound.
Values may be sent and summed in bfloat16 or wider, within the bound.
A program may use at most 128 MiB of HBM per device.

v0:
```python
import jax
import jax.numpy as jnp
from jax import lax
from jax.sharding import PartitionSpec as P

HEAD_DIM = 64


EPSILON = 1e-05
ROOT_HALF = 0.7071067811865476
INV_ROOT_TAU = 0.3989422804014327


def matmul(left, right):
    return jnp.dot(left, right, preferred_element_type=jnp.float32)


def contract_rows(left, right):
    return lax.dot_general(
        left, right, (((0,), (0,)), ((), ())), preferred_element_type=jnp.float32
    )


def contract_cols(left, right):
    return lax.dot_general(
        left, right, (((1,), (1,)), ((), ())), preferred_element_type=jnp.float32
    )


def layer_norm(residual, gain, offset):
    centre = residual - jnp.mean(residual, axis=-1, keepdims=True)
    inv_std = lax.rsqrt(jnp.mean(centre * centre, axis=-1, keepdims=True) + EPSILON)
    normed = centre * inv_std
    return (normed * gain.astype(jnp.float32) + offset.astype(jnp.float32), normed, inv_std)


def norm_grad(upstream, normed, inv_std, gain):
    scaled = upstream * gain.astype(jnp.float32)
    spread = scaled - jnp.mean(scaled, axis=-1, keepdims=True)
    return (spread - normed * jnp.mean(scaled * normed, axis=-1, keepdims=True)) * inv_std


def gelu_exact(pre_act):
    return 0.5 * pre_act * (1.0 + lax.erf(pre_act * ROOT_HALF))


def gelu_slope(pre_act):
    return (
        0.5 * (1.0 + lax.erf(pre_act * ROOT_HALF))
        + pre_act * jnp.exp(-0.5 * pre_act * pre_act) * INV_ROOT_TAU
    )


def split_heads(rows):
    return rows.reshape(rows.shape[0], rows.shape[1] // HEAD_DIM, HEAD_DIM)


def attend(query_rows, key_rows, value_rows):
    score_scale = HEAD_DIM ** (-0.5)
    query_heads = split_heads(query_rows)
    key_heads = split_heads(key_rows)
    value_heads = split_heads(value_rows)
    scores = (
        jnp.einsum("qhd,khd->hqk", query_heads, key_heads, preferred_element_type=jnp.float32)
        * score_scale
    )
    row_top = jnp.max(scores, axis=-1, keepdims=True)
    log_total = row_top + jnp.log(jnp.sum(jnp.exp(scores - row_top), axis=-1, keepdims=True))
    weights_low = jnp.exp(scores - log_total).astype(jnp.bfloat16)
    context = jnp.einsum(
        "hqk,khd->qhd", weights_low, value_heads, preferred_element_type=jnp.float32
    )
    return (context.reshape(query_rows.shape).astype(jnp.bfloat16), log_total)


def attend_back(query_rows, key_rows, value_rows, log_total, context_gradient):
    score_scale = HEAD_DIM ** (-0.5)
    row_shape = query_rows.shape
    query_heads = split_heads(query_rows)
    key_heads = split_heads(key_rows)
    value_heads = split_heads(value_rows)
    gradient_heads = split_heads(context_gradient)
    scores = (
        jnp.einsum("qhd,khd->hqk", query_heads, key_heads, preferred_element_type=jnp.float32)
        * score_scale
    )
    weights = jnp.exp(scores - log_total)
    weights_low = weights.astype(jnp.bfloat16)
    value_gradient = jnp.einsum(
        "hqk,qhd->khd", weights_low, gradient_heads, preferred_element_type=jnp.float32
    )
    prob_gradient = jnp.einsum(
        "qhd,khd->hqk", gradient_heads, value_heads, preferred_element_type=jnp.float32
    )
    score_gradient = (
        weights
        * (prob_gradient - jnp.sum(weights * prob_gradient, axis=-1, keepdims=True))
        * score_scale
    ).astype(jnp.bfloat16)
    query_gradient = jnp.einsum(
        "hqk,khd->qhd", score_gradient, key_heads, preferred_element_type=jnp.float32
    )
    key_gradient = jnp.einsum(
        "hqk,qhd->khd", score_gradient, query_heads, preferred_element_type=jnp.float32
    )
    return jnp.stack(
        [
            query_gradient.reshape(row_shape),
            key_gradient.reshape(row_shape),
            value_gradient.reshape(row_shape),
        ]
    ).astype(jnp.bfloat16)


def gather_layer(shards):
    return (
        lax.all_gather(shards[0], "fsdp", axis=0, tiled=True),
        lax.all_gather(shards[1], "fsdp", axis=0, tiled=True),
        lax.all_gather(shards[2], "fsdp", axis=0, tiled=True),
        lax.all_gather(shards[3], "fsdp", axis=0, tiled=True),
        lax.all_gather(shards[4], "fsdp", axis=0, tiled=True),
        lax.all_gather(shards[5], "fsdp", axis=0, tiled=True),
        lax.all_gather(shards[6], "fsdp", axis=0, tiled=True),
        lax.all_gather(shards[7], "fsdp", axis=0, tiled=True),
        lax.all_gather(shards[8], "fsdp", axis=0, tiled=True),
        lax.all_gather(shards[9], "fsdp", axis=0, tiled=True),
        lax.all_gather(shards[10], "fsdp", axis=0, tiled=True),
        lax.all_gather(shards[11], "fsdp", axis=0, tiled=True),
        lax.all_gather(shards[12], "fsdp", axis=0, tiled=True),
        lax.all_gather(shards[13], "fsdp", axis=0, tiled=True),
        lax.all_gather(shards[14], "fsdp", axis=0, tiled=True),
    )


def forward_layer(residual, params):
    hidden_wide, normed_in, inv_in = layer_norm(residual, params[0], params[1])
    hidden = hidden_wide.astype(jnp.bfloat16)
    query_rows = (matmul(hidden, params[2]) + params[3].astype(jnp.float32)).astype(jnp.bfloat16)
    key_rows = matmul(hidden, params[4]).astype(jnp.bfloat16)
    value_rows = (matmul(hidden, params[5]) + params[6].astype(jnp.float32)).astype(jnp.bfloat16)
    by_head = lax.all_to_all(
        jnp.stack([query_rows, key_rows, value_rows]),
        "seq",
        split_axis=2,
        concat_axis=1,
        tiled=True,
    )
    context_heads, log_total = attend(by_head[0], by_head[1], by_head[2])
    context = lax.all_to_all(context_heads, "seq", split_axis=0, concat_axis=1, tiled=True)
    middle = residual + matmul(context, params[7]) + params[8].astype(jnp.float32)
    mid_wide, normed_mid, inv_mid = layer_norm(middle, params[9], params[10])
    hidden_mid = mid_wide.astype(jnp.bfloat16)
    pre_act = matmul(hidden_mid, params[11]) + params[12].astype(jnp.float32)
    activated = gelu_exact(pre_act).astype(jnp.bfloat16)
    result = middle + matmul(activated, params[13]) + params[14].astype(jnp.float32)
    return (
        result,
        (
            hidden,
            normed_in,
            inv_in,
            by_head,
            log_total,
            context,
            normed_mid,
            inv_mid,
            hidden_mid,
            pre_act,
            activated,
        ),
    )


def backward_layer(upstream, stored, params):
    (
        hidden,
        normed_in,
        inv_in,
        by_head,
        log_total,
        context,
        normed_mid,
        inv_mid,
        hidden_mid,
        pre_act,
        activated,
    ) = stored
    upstream_low = upstream.astype(jnp.bfloat16)
    down_weight_gradient = contract_rows(activated, upstream_low)
    down_bias_gradient = jnp.sum(upstream, axis=0)
    pre_gradient = contract_cols(upstream_low, params[13]) * gelu_slope(pre_act)
    pre_low = pre_gradient.astype(jnp.bfloat16)
    up_weight_gradient = contract_rows(hidden_mid, pre_low)
    up_bias_gradient = jnp.sum(pre_gradient, axis=0)
    mid_hidden_gradient = contract_cols(pre_low, params[11])
    second_gain_gradient = jnp.sum(mid_hidden_gradient * normed_mid, axis=0)
    second_bias_gradient = jnp.sum(mid_hidden_gradient, axis=0)
    middle_gradient = upstream + norm_grad(mid_hidden_gradient, normed_mid, inv_mid, params[9])
    middle_low = middle_gradient.astype(jnp.bfloat16)
    out_weight_gradient = contract_rows(context, middle_low)
    out_bias_gradient = jnp.sum(middle_gradient, axis=0)
    context_gradient = contract_cols(middle_low, params[7]).astype(jnp.bfloat16)
    head_gradient = lax.all_to_all(context_gradient, "seq", split_axis=1, concat_axis=0, tiled=True)
    head_parts = attend_back(by_head[0], by_head[1], by_head[2], log_total, head_gradient)
    frame_parts = lax.all_to_all(head_parts, "seq", split_axis=1, concat_axis=2, tiled=True)
    query_gradient = frame_parts[0]
    key_gradient = frame_parts[1]
    value_gradient = frame_parts[2]
    query_weight_gradient = contract_rows(hidden, query_gradient)
    query_bias_gradient = jnp.sum(query_gradient.astype(jnp.float32), axis=0)
    key_weight_gradient = contract_rows(hidden, key_gradient)
    value_weight_gradient = contract_rows(hidden, value_gradient)
    value_bias_gradient = jnp.sum(value_gradient.astype(jnp.float32), axis=0)
    hidden_gradient = (
        contract_cols(query_gradient, params[2])
        + contract_cols(key_gradient, params[4])
        + contract_cols(value_gradient, params[5])
    )
    first_gain_gradient = jnp.sum(hidden_gradient * normed_in, axis=0)
    first_bias_gradient = jnp.sum(hidden_gradient, axis=0)
    input_gradient = middle_gradient + norm_grad(hidden_gradient, normed_in, inv_in, params[0])
    return (
        input_gradient,
        (
            first_gain_gradient,
            first_bias_gradient,
            query_weight_gradient,
            query_bias_gradient,
            key_weight_gradient,
            value_weight_gradient,
            value_bias_gradient,
            out_weight_gradient,
            out_bias_gradient,
            second_gain_gradient,
            second_bias_gradient,
            up_weight_gradient,
            up_bias_gradient,
            down_weight_gradient,
            down_bias_gradient,
        ),
    )


def reduce_gradients(gradients):
    shards = (
        lax.psum_scatter(gradients[0], "fsdp", scatter_dimension=0, tiled=True),
        lax.psum_scatter(gradients[1], "fsdp", scatter_dimension=0, tiled=True),
        lax.psum_scatter(gradients[2], "fsdp", scatter_dimension=0, tiled=True),
        lax.psum_scatter(gradients[3], "fsdp", scatter_dimension=0, tiled=True),
        lax.psum_scatter(gradients[4], "fsdp", scatter_dimension=0, tiled=True),
        lax.psum_scatter(gradients[5], "fsdp", scatter_dimension=0, tiled=True),
        lax.psum_scatter(gradients[6], "fsdp", scatter_dimension=0, tiled=True),
        lax.psum_scatter(gradients[7], "fsdp", scatter_dimension=0, tiled=True),
        lax.psum_scatter(gradients[8], "fsdp", scatter_dimension=0, tiled=True),
        lax.psum_scatter(gradients[9], "fsdp", scatter_dimension=0, tiled=True),
        lax.psum_scatter(gradients[10], "fsdp", scatter_dimension=0, tiled=True),
        lax.psum_scatter(gradients[11], "fsdp", scatter_dimension=0, tiled=True),
        lax.psum_scatter(gradients[12], "fsdp", scatter_dimension=0, tiled=True),
        lax.psum_scatter(gradients[13], "fsdp", scatter_dimension=0, tiled=True),
        lax.psum_scatter(gradients[14], "fsdp", scatter_dimension=0, tiled=True),
    )
    parts = (
        lax.psum_scatter(shards[0], "seq", scatter_dimension=0, tiled=True),
        lax.psum_scatter(shards[1], "seq", scatter_dimension=0, tiled=True),
        lax.psum_scatter(shards[2], "seq", scatter_dimension=0, tiled=True),
        lax.psum_scatter(shards[3], "seq", scatter_dimension=0, tiled=True),
        lax.psum_scatter(shards[4], "seq", scatter_dimension=0, tiled=True),
        lax.psum_scatter(shards[5], "seq", scatter_dimension=0, tiled=True),
        lax.psum_scatter(shards[6], "seq", scatter_dimension=0, tiled=True),
        lax.psum_scatter(shards[7], "seq", scatter_dimension=0, tiled=True),
        lax.psum_scatter(shards[8], "seq", scatter_dimension=0, tiled=True),
        lax.psum_scatter(shards[9], "seq", scatter_dimension=0, tiled=True),
        lax.psum_scatter(shards[10], "seq", scatter_dimension=0, tiled=True),
        lax.psum_scatter(shards[11], "seq", scatter_dimension=0, tiled=True),
        lax.psum_scatter(shards[12], "seq", scatter_dimension=0, tiled=True),
        lax.psum_scatter(shards[13], "seq", scatter_dimension=0, tiled=True),
        lax.psum_scatter(shards[14], "seq", scatter_dimension=0, tiled=True),
    )
    return (
        lax.all_gather(parts[0], "seq", axis=0, tiled=True),
        lax.all_gather(parts[1], "seq", axis=0, tiled=True),
        lax.all_gather(parts[2], "seq", axis=0, tiled=True),
        lax.all_gather(parts[3], "seq", axis=0, tiled=True),
        lax.all_gather(parts[4], "seq", axis=0, tiled=True),
        lax.all_gather(parts[5], "seq", axis=0, tiled=True),
        lax.all_gather(parts[6], "seq", axis=0, tiled=True),
        lax.all_gather(parts[7], "seq", axis=0, tiled=True),
        lax.all_gather(parts[8], "seq", axis=0, tiled=True),
        lax.all_gather(parts[9], "seq", axis=0, tiled=True),
        lax.all_gather(parts[10], "seq", axis=0, tiled=True),
        lax.all_gather(parts[11], "seq", axis=0, tiled=True),
        lax.all_gather(parts[12], "seq", axis=0, tiled=True),
        lax.all_gather(parts[13], "seq", axis=0, tiled=True),
        lax.all_gather(parts[14], "seq", axis=0, tiled=True),
    )


def on_device(
    frames_in,
    cotangent,
    first_gain,
    first_bias,
    query_weight,
    query_bias,
    key_weight,
    value_weight,
    value_bias,
    out_weight,
    out_bias,
    second_gain,
    second_bias,
    up_weight,
    up_bias,
    down_weight,
    down_bias,
):
    stacks = (
        first_gain,
        first_bias,
        query_weight,
        query_bias,
        key_weight,
        value_weight,
        value_bias,
        out_weight,
        out_bias,
        second_gain,
        second_bias,
        up_weight,
        up_bias,
        down_weight,
        down_bias,
    )
    layer_count = first_gain.shape[0]
    residual = frames_in[0]
    layer_num = 0
    params = gather_layer([stack[layer_num] for stack in stacks])
    residual, stored = forward_layer(residual, params)
    stored_all = [stored]
    gathered = [params]
    upstream = cotangent[0]
    reduced = [None] * layer_count
    for layer_num in reversed(range(layer_count)):
        params = gathered[layer_num]
        upstream, gradients = backward_layer(upstream, stored_all[layer_num], params)
        reduced[layer_num] = reduce_gradients(gradients)
    results = [residual[None], upstream[None]]
    for member in range(len(stacks)):
        results.append(jnp.stack([reduced[0][member]]))
    return tuple(results)


def solution(mesh):
    return jax.shard_map(
        on_device,
        mesh=mesh,
        in_specs=(
            P("fsdp", "seq", None),
            P("fsdp", "seq", None),
            P(None, "fsdp"),
            P(None, "fsdp"),
            P(None, "fsdp", None),
            P(None, "fsdp"),
            P(None, "fsdp", None),
            P(None, "fsdp", None),
            P(None, "fsdp"),
            P(None, "fsdp", None),
            P(None, "fsdp"),
            P(None, "fsdp"),
            P(None, "fsdp"),
            P(None, "fsdp", None),
            P(None, "fsdp"),
            P(None, "fsdp", None),
            P(None, "fsdp"),
        ),
        out_specs=(
            P("fsdp", "seq", None),
            P("fsdp", "seq", None),
            P(None, "fsdp"),
            P(None, "fsdp"),
            P(None, "fsdp", None),
            P(None, "fsdp"),
            P(None, "fsdp", None),
            P(None, "fsdp", None),
            P(None, "fsdp"),
            P(None, "fsdp", None),
            P(None, "fsdp"),
            P(None, "fsdp"),
            P(None, "fsdp"),
            P(None, "fsdp", None),
            P(None, "fsdp"),
            P(None, "fsdp", None),
            P(None, "fsdp"),
        ),
        check_vma=False,
    )
```

profile of v0, /device:TPU:0, one launch (start us, length us, event | category | flops | bytes accessed | tf_op | source)
XLA Modules:
  0.0 885.4 jit_solution(2830720401970173773)
XLA Ops:
  21.5 63.2 %all-reduce.39 = (bf16[768]{0:T(1024)(128)(2,1)S(1)}, bf16[768]{0:T(1024)(128)(2,1)S(1)}, bf16[768]{0:T(1024)(128)(2,1)S(1)}, bf16[768]{0:T(1024)(128)(2,1)S(1)}...) all-reduce(bf16[768]{0:T(1024)(128)(2,1)S(1)} %dynamic-update-slice, ...), channel_id=3, replica_groups=mesh['seq'=2,'fsdp'=16] {'fsdp'}, use_global_device_ids=true, to_apply=%add.1 | all-reduce | flops 9216 | bytes 36864
  92.5 37.9 %all-gather.22.cloned.1.call-done = bf16[1,768,768]{2,1,0:T(8,128)(2,1)} async-done(((bf16[1,48,768]{2,1,0:T(8,128)(2,1)}), bf16[1,768,768]{2,1,0:T(8,128)(2,1)}) %all-gather.22.cloned.1.call-update) | async-done | bytes 1179664 | tf_op jit(solution)/shard_map/all_gather | solution.py:119
  132.7 13.9 %all_to_all.62 = bf16[3,128,768]{1,0,2:T(4,128)(2,1)S(1)} all-to-all(bf16[3,128,768]{1,0,2:T(4,128)(2,1)S(1)} %copy.66), channel_id=1, replica_groups=mesh['seq'=2,'fsdp'=16] {'seq'}, dimensions={2} | all-to-all | bytes 1179648 | tf_op jit(solution)/shard_map/all_to_all | solution.py:141
  154.1 15.5 %all-gather.28.cloned.1.call-done = bf16[1,768,768]{2,1,0:T(8,128)(2,1)} async-done(((bf16[1,48,768]{2,1,0:T(8,128)(2,1)}), bf16[1,768,768]{2,1,0:T(8,128)(2,1)}) %all-gather.28.cloned.1.call-update) | async-done | bytes 1179664 | tf_op jit(solution)/shard_map/all_gather | solution.py:124
  171.6 52.2 %all-gather.30.cloned.1.call-done = bf16[1,768,3072]{2,1,0:T(8,128)(2,1)} async-done(((bf16[1,48,3072]{2,1,0:T(8,128)(2,1)}), bf16[1,768,3072]{2,1,0:T(8,128)(2,1)}) %all-gather.30.cloned.1.call-update) | async-done | bytes 4718608 | tf_op jit(solution)/shard_map/all_gather | solution.py:128
  223.8 4.4 fusion.9
  228.1 49.5 %all-gather.32.cloned.1.call-done = bf16[1,3072,768]{2,1,0:T(8,128)(2,1)} async-done(((bf16[1,192,768]{2,1,0:T(8,128)(2,1)}), bf16[1,3072,768]{2,1,0:T(8,128)(2,1)}) %all-gather.32.cloned.1.call-update) | async-done | bytes 4718608 | tf_op jit(solution)/shard_map/all_gather | solution.py:130
  277.6 5.3 fusion.108
  290.6 7.5 all_to_all.63
  316.1 12.9 %all_to_all.64 = bf16[3,256,384]{2,0,1:T(4,128)(2,1)S(1)} all-to-all(bf16[3,256,384]{2,0,1:T(4,128)(2,1)S(1)} %pad_maximum_fusion), channel_id=1, replica_groups=mesh['seq'=2,'fsdp'=16] {'seq'}, dimensions={1} | all-to-all | bytes 1179648 | tf_op jit(solution)/shard_map/all_to_all | solution.py:205
  338.0 5.2 fusion.84
  344.6 5.1 fusion.91
  350.6 65.9 %reduce-scatter.13.cloned.1.call-done = f32[48,768]{1,0:T(8,128)} async-done(((f32[768,768]{1,0:T(8,128)}), f32[48,768]{1,0:T(8,128)}) %reduce-scatter.13.cloned.1.call-update) | async-done | bytes 147472 | tf_op jit(solution)/shard_map/reduce_scatter | solution.py:248
  420.6 62.0 %reduce-scatter.17.cloned.1.call-done = f32[48,768]{1,0:T(8,128)} async-done(((f32[768,768]{1,0:T(8,128)}), f32[48,768]{1,0:T(8,128)}) %reduce-scatter.17.cloned.1.call-update) | async-done | bytes 147472 | tf_op jit(solution)/shard_map/reduce_scatter | solution.py:250
  486.6 61.8 %reduce-scatter.21.cloned.1.call-done = f32[48,768]{1,0:T(8,128)} async-done(((f32[768,768]{1,0:T(8,128)}), f32[48,768]{1,0:T(8,128)}) %reduce-scatter.21.cloned.1.call-update) | async-done | bytes 147472 | tf_op jit(solution)/shard_map/reduce_scatter | solution.py:251
  552.7 110.2 %reduce-scatter.29.cloned.1.call-done = f32[48,3072]{1,0:T(8,128)} async-done(((f32[768,3072]{1,0:T(8,128)}), f32[48,3072]{1,0:T(8,128)}) %reduce-scatter.29.cloned.1.call-update) | async-done | bytes 589840 | tf_op jit(solution)/shard_map/reduce_scatter | solution.py:257
  665.8 62.5 %all-reduce.36 = (f32[768]{0:T(1024)S(1)}, f32[768]{0:T(1024)S(1)}, f32[768]{0:T(1024)S(1)}, f32[768]{0:T(1024)S(1)}, f32[768]{0:T(1024)S(1)}, /*index=5*/f32[76...) all-reduce(f32[768]{0:T(1024)S(1)} %get-tuple-element.19, ...), channel_id=17, replica_groups=mesh['seq'=2,'fsdp'=16] {'fsdp'}, use_global_device_ids=true, to_apply=%region_12.0.clone | all-reduce | flops 9216 | bytes 73728
  729.0 5.0 all-reduce.38
  735.1 44.5 %reduce-scatter.33.cloned.1.call-done = f32[192,768]{1,0:T(8,128)} async-done(((f32[3072,768]{1,0:T(8,128)}), f32[192,768]{1,0:T(8,128)}) %reduce-scatter.33.cloned.1.call-update) | async-done | bytes 589840 | tf_op jit(solution)/shard_map/reduce_scatter | solution.py:259
  779.9 5.5 all-reduce.37
  786.4 5.6 reduce-scatter.27.cloned.1.call-done
  792.0 5.2 all_gather.112
  797.2 7.4 reduce-scatter.15.cloned.1.call-done
  804.6 5.2 all_gather.107
  809.8 7.4 reduce-scatter.19.cloned.1.call-done
  817.2 5.2 all_gather.109
  822.5 7.4 reduce-scatter.23.cloned.1.call-done
  829.9 5.2 all_gather.110
  835.1 12.3 %reduce-scatter.31.cloned.1.call-done = f32[24,3072]{1,0:T(8,128)} async-done(((f32[48,3072]{1,0:T(8,128)}), f32[24,3072]{1,0:T(8,128)}) %reduce-scatter.31.cloned.1.call-update) | async-done | bytes 294928 | tf_op jit(solution)/shard_map/reduce_scatter | solution.py:274
  847.3 9.5 %all_gather.116 = f32[48,3072]{1,0:T(8,128)S(1)} all-gather(f32[24,3072]{1,0:T(8,128)} %reduce-scatter.31.cloned.1.call-done), channel_id=1, replica_groups=mesh['seq'=2,'fsdp'=16] {'seq'}, dimensions={0}, use_global_device_ids=true | all-gather | bytes 884736 | tf_op jit(solution)/shard_map/all_gather | solution.py:291
  856.8 8.0 reduce-scatter.35.cloned.1.call-done
  864.9 9.5 %all_gather.118 = f32[192,768]{1,0:T(8,128)S(1)} all-gather(f32[96,768]{1,0:T(8,128)} %reduce-scatter.35.cloned.1.call-done), channel_id=1, replica_groups=mesh['seq'=2,'fsdp'=16] {'seq'}, dimensions={0}, use_global_device_ids=true | all-gather | bytes 884736 | tf_op jit(solution)/shard_map/all_gather | solution.py:293
  (221 shorter events, 87.6 us)
Async XLA Ops:
  7.2 78.6 %copy-start = (f32[1,128,768]{2,1,0:T(8,128)S(1)}, f32[1,128,768]{2,1,0:T(8,128)}, u32[]{:S(2)}) copy-start(f32[1,128,768]{2,1,0:T(8,128)} %param.17) | copy-start | bytes 1179652
  7.2 78.9 %all-gather.24.cloned.1.call-start = ((), (), s32[]{:S(2)}) async-start(), calls=%async_computation.29 | async-start | bytes 1253376 | tf_op jit(solution)/shard_map/all_gather | solution.py:121
  7.9 82.9 %all-gather.26.cloned.1.call-start = ((), (), s32[]{:S(2)}) async-start(), calls=%async_computation.30 | async-start | bytes 1253376 | tf_op jit(solution)/shard_map/all_gather | solution.py:122
  8.7 121.7 %all-gather.22.cloned.1.call-start = ((), (), s32[]{:S(2)}) async-start(), calls=%async_computation.28 | async-start | bytes 1253376 | tf_op jit(solution)/shard_map/all_gather | solution.py:119
  9.4 160.2 %all-gather.28.cloned.1.call-start = ((), (), s32[]{:S(2)}) async-start(), calls=%async_computation.31 | async-start | bytes 1253376 | tf_op jit(solution)/shard_map/all_gather | solution.py:124
  10.0 213.8 %all-gather.30.cloned.1.call-start = ((), (), s32[]{:S(2)}) async-start(), calls=%async_computation.32 | async-start | bytes 5013504 | tf_op jit(solution)/shard_map/all_gather | solution.py:128
  10.6 267.0 %all-gather.32.cloned.1.call-start = ((), (), s32[]{:S(2)}) async-start(), calls=%async_computation.33 | async-start | bytes 5013504 | tf_op jit(solution)/shard_map/all_gather | solution.py:130
  85.8 44.5 %copy-start.14 = (f32[128]{0:T(128)}, f32[128]{0:T(128)S(1)}, u32[]{:S(2)}) copy-start(f32[128]{0:T(128)S(1)} %broadcast_multiply_fusion.5) | copy-start | bytes 1540
  86.0 44.3 %copy-start.17 = (f32[128]{0:T(128)}, f32[128]{0:T(128)S(1)}, u32[]{:S(2)}) copy-start(f32[128]{0:T(128)S(1)} %add_rsqrt_fusion.1) | copy-start | bytes 1540
  150.6 19.0 %all-to-all-start.1 = ((bf16[2,128,384]{1,2,0:T(8,128)(2,1)}), bf16[2,128,384]{1,2,0:T(8,128)(2,1)S(1)}, u32[]{:S(2)}, u32[]{:S(2)}) async-start(bf16[2,128,384]{1,2,0:T(8,128)(2,1)} %copy.69), calls=%async_computation.1 | async-start | bytes 393216 | tf_op jit(solution)/shard_map/all_to_all | solution.py:149
  154.0 196.5 %reduce-scatter.25.cloned.1.call-start = ((), (), s32[]{:S(2)}) async-start(), calls=%async_computation.22 | async-start | bytes 2506752 | tf_op jit(solution)/shard_map/reduce_scatter | solution.py:253
  171.3 111.6 %copy-start.20 = (f32[128]{0:T(128)}, f32[128]{0:T(128)S(1)}, u32[]{:S(2)}) copy-start(f32[128]{0:T(128)S(1)} %broadcast_multiply_fusion.4) | copy-start | bytes 1540
  171.5 111.4 %copy-start.25 = (f32[128]{0:T(128)}, f32[128]{0:T(128)S(1)}, u32[]{:S(2)}) copy-start(f32[128]{0:T(128)S(1)} %add_rsqrt_fusion) | copy-start | bytes 1540
  171.5 106.1 %copy-start.6 = (f32[1,128,768]{2,1,0:T(8,128)S(1)}, f32[1,128,768]{2,1,0:T(8,128)}, u32[]{:S(2)}) copy-start(f32[1,128,768]{2,1,0:T(8,128)} %param.18) | copy-start | bytes 1179652
  277.6 5.3 copy-start.2
  288.7 127.9 %reduce-scatter.13.cloned.1.call-start = ((), (), s32[]{:S(2)}) async-start(), calls=%async_computation.16 | async-start | bytes 2506752 | tf_op jit(solution)/shard_map/reduce_scatter | solution.py:248
  309.0 4.7 copy-start.10
  332.2 150.4 %reduce-scatter.17.cloned.1.call-start = ((), (), s32[]{:S(2)}) async-start(), calls=%async_computation.18 | async-start | bytes 2506752 | tf_op jit(solution)/shard_map/reduce_scatter | solution.py:250
  334.6 213.9 %reduce-scatter.21.cloned.1.call-start = ((), (), s32[]{:S(2)}) async-start(), calls=%async_computation.20 | async-start | bytes 2506752 | tf_op jit(solution)/shard_map/reduce_scatter | solution.py:251
  336.9 326.0 %reduce-scatter.29.cloned.1.call-start = ((), (), s32[]{:S(2)}) async-start(), calls=%async_computation.24 | async-start | bytes 10027008 | tf_op jit(solution)/shard_map/reduce_scatter | solution.py:257
  343.2 436.4 %reduce-scatter.33.cloned.1.call-start = ((), (), s32[]{:S(2)}) async-start(), calls=%async_computation.26 | async-start | bytes 10027008 | tf_op jit(solution)/shard_map/reduce_scatter | solution.py:259
  349.6 67.0 %copy-start.28 = (bf16[768]{0:T(1024)(128)(2,1)S(1)}, bf16[768]{0:T(1024)(128)(2,1)}, u32[]{:S(2)}) copy-start(bf16[768]{0:T(1024)(128)(2,1)} %get-tuple-element.59) | copy-start | bytes 4612
  349.6 442.4 %reduce-scatter.27.cloned.1.call-start = ((), (), s32[]{:S(2)}) async-start(), calls=%async_computation.23 | async-start | bytes 221184 | tf_op jit(solution)/shard_map/reduce_scatter | solution.py:270
  350.6 454.0 %reduce-scatter.15.cloned.1.call-start = ((), (), s32[]{:S(2)}) async-start(), calls=%async_computation.17 | async-start | bytes 221184 | tf_op jit(solution)/shard_map/reduce_scatter | solution.py:265
  416.6 400.6 %reduce-scatter.19.cloned.1.call-start = ((), (), s32[]{:S(2)}) async-start(), calls=%async_computation.19 | async-start | bytes 221184 | tf_op jit(solution)/shard_map/reduce_scatter | solution.py:267
  482.6 347.2 %reduce-scatter.23.cloned.1.call-start = ((), (), s32[]{:S(2)}) async-start(), calls=%async_computation.21 | async-start | bytes 221184 | tf_op jit(solution)/shard_map/reduce_scatter | solution.py:268
  486.6 63.7 %copy-start.4 = (bf16[1,768,768]{2,1,0:T(8,128)(2,1)S(1)}, bf16[1,768,768]{2,1,0:T(8,128)(2,1)}, u32[]{:S(2)}) copy-start(bf16[1,768,768]{2,1,0:T(8,128)(2,1)} %all-gather.24.cloned.1.call-done) | copy-start | bytes 3538948
  548.5 298.9 %reduce-scatter.31.cloned.1.call-start = ((), (), s32[]{:S(2)}) async-start(), calls=%async_computation.25 | async-start | bytes 884736 | tf_op jit(solution)/shard_map/reduce_scatter | solution.py:274
  550.4 113.7 %copy-start.3 = (bf16[1,768,768]{2,1,0:T(8,128)(2,1)S(1)}, bf16[1,768,768]{2,1,0:T(8,128)(2,1)}, u32[]{:S(2)}) copy-start(bf16[1,768,768]{2,1,0:T(8,128)(2,1)} %all-gather.26.cloned.1.call-done) | copy-start | bytes 3538948
  550.4 113.7 %copy-start.16 = (f32[128]{0:T(128)S(1)}, f32[128]{0:T(128)}, u32[]{:S(2)}) copy-start(f32[128]{0:T(128)} %copy-done.14) | copy-start | bytes 1540
  550.4 113.7 %copy-start.19 = (f32[128]{0:T(128)S(1)}, f32[128]{0:T(128)}, u32[]{:S(2)}) copy-start(f32[128]{0:T(128)} %copy-done.17) | copy-start | bytes 1540
  662.9 201.9 %reduce-scatter.35.cloned.1.call-start = ((), (), s32[]{:S(2)}) async-start(), calls=%async_computation.27 | async-start | bytes 884736 | tf_op jit(solution)/shard_map/reduce_scatter | solution.py:276
  (16 other events, 26.2 us)
Sparse Core Ops, SparseCore 0:
  10.3 41.0 all-gather.23
  53.7 37.1 all-gather.25
  93.1 37.1 all-gather.21
  132.5 37.0 all-gather.27
  171.7 51.9 all-gather.29
  225.9 51.6 all-gather.31
  288.8 61.7 reduce-scatter.24
  354.3 62.1 reduce-scatter.12
  420.3 62.1 reduce-scatter.16
  486.2 62.2 reduce-scatter.20
  552.6 110.2 reduce-scatter.28
  666.8 112.7 reduce-scatter.32
  781.8 10.1 reduce-scatter.26
  794.1 10.5 reduce-scatter.14
  806.7 10.5 reduce-scatter.18
  819.3 10.5 reduce-scatter.22
  832.0 15.3 reduce-scatter.30
  849.5 15.3 reduce-scatter.34
where the time goes:
time: 887 us; the launch traced here: 885 us
  waiting for transfers between devices  555 us (63%)
  blocking collectives  210 us (24%)
  matrix products  58.7 us (7%)
  local copies, waits for them, and re-layouts  28.3 us (3%)
  between operations  20.1 us (2%)
    unnamed x4, blocking collectives  136 us
    reduce_scatter x1, waiting for transfers between devices, reduce_gradients(): lax.psum_scatter(gradients[11], 'fsdp', scatter_dimension=0, tiled=True)  110 us
    reduce_scatter x1, waiting for transfers between devices, reduce_gradients(): lax.psum_scatter(gradients[2], 'fsdp', scatter_dimension=0, tiled=True)  65.9 us
    reduce_scatter x1, waiting for transfers between devices, reduce_gradients(): lax.psum_scatter(gradients[4], 'fsdp', scatter_dimension=0, tiled=True)  62 us
    reduce_scatter x1, waiting for transfers between devices, reduce_gradients(): lax.psum_scatter(gradients[5], 'fsdp', scatter_dimension=0, tiled=True)  61.8 us
    all_gather x1, waiting for transfers between devices, gather_layer(): lax.all_gather(shards[11], 'fsdp', axis=0, tiled=True)  52.2 us
    all_gather x1, waiting for transfers between devices, gather_layer(): lax.all_gather(shards[13], 'fsdp', axis=0, tiled=True)  49.5 us
    reduce_scatter x1, waiting for transfers between devices, reduce_gradients(): lax.psum_scatter(gradients[13], 'fsdp', scatter_dimension=0, tiled=True)  44.5 us
  transfers between devices with their start and end apart: 19, of which 17 were waited for; matrix products, arithmetic and copies ran while one was open for 9% of the time, Pallas kernels for 0%

commit v1 on v0

v1 whole, which is shorter than its diff:
```python
import jax
import jax.numpy as jnp
from jax import lax
from jax.sharding import PartitionSpec as P

HEAD_DIM = 64


EPSILON = 1e-05
ROOT_HALF = 0.7071067811865476
INV_ROOT_TAU = 0.3989422804014327


def matmul(left, right):
    return jnp.dot(left, right, preferred_element_type=jnp.float32)


def contract_rows(left, right):
    return lax.dot_general(
        left, right, (((0,), (0,)), ((), ())), preferred_element_type=jnp.float32
    )


def contract_cols(left, right):
    return lax.dot_general(
        left, right, (((1,), (1,)), ((), ())), preferred_element_type=jnp.float32
    )


def layer_norm(residual, gain, offset):
    centre = residual - jnp.mean(residual, axis=-1, keepdims=True)
    inv_std = lax.rsqrt(jnp.mean(centre * centre, axis=-1, keepdims=True) + EPSILON)
    normed = centre * inv_std
    return (normed * gain.astype(jnp.float32) + offset.astype(jnp.float32), normed, inv_std)


def norm_grad(upstream, normed, inv_std, gain):
    scaled = upstream * gain.astype(jnp.float32)
    spread = scaled - jnp.mean(scaled, axis=-1, keepdims=True)
    return (spread - normed * jnp.mean(scaled * normed, axis=-1, keepdims=True)) * inv_std


def gelu_exact(pre_act):
    return 0.5 * pre_act * (1.0 + lax.erf(pre_act * ROOT_HALF))


def gelu_slope(pre_act):
    return (
        0.5 * (1.0 + lax.erf(pre_act * ROOT_HALF))
        + pre_act * jnp.exp(-0.5 * pre_act * pre_act) * INV_ROOT_TAU
    )


def split_heads(rows):
    return rows.reshape(rows.shape[0], rows.shape[1] // HEAD_DIM, HEAD_DIM)


def attend(query_rows, key_rows, value_rows):
    score_scale = HEAD_DIM ** (-0.5)
    query_heads = split_heads(query_rows)
    key_heads = split_heads(key_rows)
    value_heads = split_heads(value_rows)
    scores = (
        jnp.einsum("qhd,khd->hqk", query_heads, key_heads, preferred_element_type=jnp.float32)
        * score_scale
    )
    row_top = jnp.max(scores, axis=-1, keepdims=True)
    log_total = row_top + jnp.log(jnp.sum(jnp.exp(scores - row_top), axis=-1, keepdims=True))
    weights = jnp.exp(scores - log_total)
    context = jnp.einsum(
        "hqk,khd->qhd",
        weights.astype(jnp.bfloat16),
        value_heads,
        preferred_element_type=jnp.float32,
    )
    return (context.reshape(query_rows.shape).astype(jnp.bfloat16), weights)


def attend_back(query_rows, key_rows, value_rows, weights, context_gradient):
    score_scale = HEAD_DIM ** (-0.5)
    row_shape = query_rows.shape
    query_heads = split_heads(query_rows)
    key_heads = split_heads(key_rows)
    value_heads = split_heads(value_rows)
    gradient_heads = split_heads(context_gradient)
    value_gradient = jnp.einsum(
        "hqk,qhd->khd",
        weights.astype(jnp.bfloat16),
        gradient_heads,
        preferred_element_type=jnp.float32,
    )
    prob_gradient = jnp.einsum(
        "qhd,khd->hqk", gradient_heads, value_heads, preferred_element_type=jnp.float32
    )
    score_gradient = (
        weights
        * (prob_gradient - jnp.sum(weights * prob_gradient, axis=-1, keepdims=True))
        * score_scale
    ).astype(jnp.bfloat16)
    query_gradient = jnp.einsum(
        "hqk,khd->qhd", score_gradient, key_heads, preferred_element_type=jnp.float32
    )
    key_gradient = jnp.einsum(
        "hqk,qhd->khd", score_gradient, query_heads, preferred_element_type=jnp.float32
    )
    return tuple(
        part.reshape(row_shape).astype(jnp.bfloat16)
        for part in (query_gradient, key_gradient, value_gradient)
    )


VECTORS = (0, 1, 3, 6, 8, 9, 10, 12, 14)
MATRICES = (2, 4, 5, 7, 11, 13)
PAD_ROWS = 16


def cut_columns(rows, width):
    blocks = rows.shape[-1] // width
    if blocks == 1:
        return rows
    return jnp.concatenate(
        [rows[..., i * width : (i + 1) * width] for i in range(blocks)], axis=-2
    )


def join_columns(rows, blocks):
    if blocks == 1:
        return rows
    size = rows.shape[-2] // blocks
    return jnp.concatenate(
        [rows[..., i * size : (i + 1) * size, :] for i in range(blocks)], axis=-1
    )


def gather_layer(shards, width):
    pieces = [cut_columns(shards[i], width) for i in MATRICES]
    vector = jnp.concatenate([shards[i] for i in VECTORS])
    vector = jnp.pad(vector, (0, PAD_ROWS * width - vector.shape[0]))
    pieces.append(vector.reshape(PAD_ROWS, width))
    packed = lax.all_gather(jnp.concatenate(pieces, axis=0), "fsdp", axis=0, tiled=False)
    params = [None] * len(shards)
    start = 0
    for i in MATRICES:
        blocks = shards[i].shape[1] // width
        size = shards[i].shape[0] * blocks
        part = join_columns(packed[:, start : start + size], blocks)
        params[i] = part.reshape(-1, shards[i].shape[1])
        start += size
    vectors = packed[:, start:].reshape(packed.shape[0], -1)
    start = 0
    for i in VECTORS:
        size = shards[i].shape[0]
        params[i] = vectors[:, start : start + size].reshape(-1)
        start += size
    return params


def reduce_gradients(gradients, shards, width, seq_size, seq_index, fsdp_size):
    part_width = width // seq_size
    pieces = []
    for i in MATRICES:
        blocks = shards[i].shape[1] // width
        rows = gradients[i].astype(jnp.bfloat16)
        rows = rows.reshape(fsdp_size, shards[i].shape[0], rows.shape[1])
        pieces.append(cut_columns(rows, part_width))
    vector = jnp.concatenate(
        [gradients[i].reshape(fsdp_size, -1) for i in VECTORS], axis=1
    ).astype(jnp.bfloat16)
    vector = jnp.pad(vector, ((0, 0), (0, PAD_ROWS * width - vector.shape[1])))
    vector = vector.reshape(fsdp_size, PAD_ROWS * seq_size, part_width)
    pieces.append(lax.dynamic_slice_in_dim(vector, seq_index * PAD_ROWS, PAD_ROWS, axis=1))
    packed = jnp.concatenate(pieces, axis=1)
    mine = lax.psum_scatter(packed, "fsdp", scatter_dimension=0, tiled=False)
    both = lax.all_gather(mine, "seq", axis=0, tiled=False)
    reduced = [None] * len(shards)
    start = 0
    for i in MATRICES:
        blocks = shards[i].shape[1] // width
        size = shards[i].shape[0] * blocks
        part = join_columns(both[:, start : start + size], blocks)
        whole = jnp.concatenate([part[s] for s in range(seq_size)], axis=-1)
        reduced[i] = whole.astype(jnp.float32)[None]
        start += size
    vector = both[:, start:].reshape(-1).astype(jnp.float32)
    start = 0
    for i in VECTORS:
        size = shards[i].shape[0]
        reduced[i] = vector[start : start + size][None]
        start += size
    return reduced


def on_device(frames_in, cotangent, *stacks):
    width = frames_in.shape[2]
    seq_size = lax.axis_size("seq")
    seq_index = lax.axis_index("seq")
    fsdp_size = lax.axis_size("fsdp")
    shards = [stack[0] for stack in stacks]
    own = frames_in.shape[1]

    mine = jnp.stack([frames_in[0], cotangent[0]])
    if seq_size == 2:
        other = lax.ppermute(mine, "seq", [(0, 1), (1, 0)])
        first = seq_index == 0
        rows = jnp.concatenate(
            [jnp.where(first, mine, other), jnp.where(first, other, mine)], axis=1
        )
    else:
        rows = lax.all_gather(mine, "seq", axis=1, tiled=True)
    residual, upstream = rows[0], rows[1]
    params = gather_layer(shards, width)

    def own_columns(matrix):
        size = matrix.shape[1] // seq_size
        return lax.dynamic_slice_in_dim(matrix, seq_index * size, size, axis=1)

    def own_rows(matrix):
        return lax.dynamic_slice_in_dim(matrix, seq_index * own, own, axis=0)[None]

    wide = [None if i in MATRICES else p.astype(jnp.float32) for i, p in enumerate(params)]

    hidden_wide, normed_in, inv_in = layer_norm(residual, params[0], params[1])
    hidden = hidden_wide.astype(jnp.bfloat16)
    query_rows = (matmul(hidden, params[2]) + wide[3]).astype(jnp.bfloat16)
    key_rows = matmul(hidden, params[4]).astype(jnp.bfloat16)
    value_rows = (matmul(hidden, params[5]) + wide[6]).astype(jnp.bfloat16)
    context, weights = attend(query_rows, key_rows, value_rows)
    middle = residual + matmul(context, params[7]) + wide[8]
    mid_wide, normed_mid, inv_mid = layer_norm(middle, params[9], params[10])
    hidden_mid = mid_wide.astype(jnp.bfloat16)
    pre_act = matmul(hidden_mid, params[11]) + wide[12]
    activated = gelu_exact(pre_act).astype(jnp.bfloat16)
    own_activated = own_rows(activated)[0]
    outputs = own_rows(middle)[0] + matmul(own_activated, params[13]) + wide[14]

    gradients = [None] * len(stacks)
    upstream_low = upstream.astype(jnp.bfloat16)
    gradients[13] = contract_rows(activated, own_columns(upstream_low))
    gradients[14] = jnp.sum(upstream, axis=0)
    pre_gradient = contract_cols(upstream_low, params[13]) * gelu_slope(pre_act)
    pre_low = pre_gradient.astype(jnp.bfloat16)
    gradients[11] = contract_rows(hidden_mid, own_columns(pre_low))
    gradients[12] = jnp.sum(pre_gradient, axis=0)
    mid_hidden_gradient = contract_cols(pre_low, params[11])
    gradients[9] = jnp.sum(mid_hidden_gradient * normed_mid, axis=0)
    gradients[10] = jnp.sum(mid_hidden_gradient, axis=0)
    middle_gradient = upstream + norm_grad(mid_hidden_gradient, normed_mid, inv_mid, params[9])
    middle_low = middle_gradient.astype(jnp.bfloat16)
    gradients[7] = contract_rows(context, own_columns(middle_low))
    gradients[8] = jnp.sum(middle_gradient, axis=0)
    context_gradient = contract_cols(middle_low, params[7]).astype(jnp.bfloat16)
    query_gradient, key_gradient, value_gradient = attend_back(
        query_rows, key_rows, value_rows, weights, context_gradient
    )
    gradients[2] = contract_rows(hidden, own_columns(query_gradient))
    gradients[3] = jnp.sum(query_gradient.astype(jnp.float32), axis=0)
    gradients[4] = contract_rows(hidden, own_columns(key_gradient))
    gradients[5] = contract_rows(hidden, own_columns(value_gradient))
    gradients[6] = jnp.sum(value_gradient.astype(jnp.float32), axis=0)
    hidden_gradient = (
        contract_cols(query_gradient, params[2])
        + contract_cols(key_gradient, params[4])
        + contract_cols(value_gradient, params[5])
    )
    gradients[0] = jnp.sum(hidden_gradient * normed_in, axis=0)
    gradients[1] = jnp.sum(hidden_gradient, axis=0)
    input_gradient = middle_gradient + norm_grad(hidden_gradient, normed_in, inv_in, params[0])
    reduced = reduce_gradients(gradients, shards, width, seq_size, seq_index, fsdp_size)
    return (outputs[None], own_rows(input_gradient), *reduced)


def solution(mesh):
    return jax.shard_map(
        on_device,
        mesh=mesh,
        in_specs=(
            P("fsdp", "seq", None),
            P("fsdp", "seq", None),
            P(None, "fsdp"),
            P(None, "fsdp"),
            P(None, "fsdp", None),
            P(None, "fsdp"),
            P(None, "fsdp", None),
            P(None, "fsdp", None),
            P(None, "fsdp"),
            P(None, "fsdp", None),
            P(None, "fsdp"),
            P(None, "fsdp"),
            P(None, "fsdp"),
            P(None, "fsdp", None),
            P(None, "fsdp"),
            P(None, "fsdp", None),
            P(None, "fsdp"),
        ),
        out_specs=(
            P("fsdp", "seq", None),
            P("fsdp", "seq", None),
            P(None, "fsdp"),
            P(None, "fsdp"),
            P(None, "fsdp", None),
            P(None, "fsdp"),
            P(None, "fsdp", None),
            P(None, "fsdp", None),
            P(None, "fsdp"),
            P(None, "fsdp", None),
            P(None, "fsdp"),
            P(None, "fsdp"),
            P(None, "fsdp"),
            P(None, "fsdp", None),
            P(None, "fsdp"),
            P(None, "fsdp", None),
            P(None, "fsdp"),
        ),
        check_vma=False,
    )
```

time: 887 us -> 334 us (0.38)
  waiting for transfers between devices: 555 us -> 191 us
  blocking collectives: 210 us -> 12.2 us
  local copies, waits for them, and re-layouts: 28.3 us -> 54.3 us
  matrix products: 58.7 us -> 44.1 us
    reduce_scatter x12 -> x1, waiting for transfers between devices: 393 us -> 81.6 us  [reduce_gradients(): mine = lax.psum_scatter(packed, 'fsdp', scatter_dimension=0, tiled=False)]
    unnamed x4 -> x0, blocking collectives: 136 us -> none
    all_gather x6 -> x1, waiting for transfers between devices: 158 us -> 91.6 us  [gather_layer(): lax.all_gather(jnp.concatenate(pieces, axis=0), 'fsdp', axis=0, tiled=False)]
    all_to_all x3 -> x0, blocking collectives: 34.3 us -> none  [the longest x1 13.9 us: forward_layer(): lax.all_to_all(jnp.stack([query_rows, key_rows, value_rows]), 'seq', spli...]
    all_gather x6 -> x1, blocking collectives: 39.8 us -> 12.2 us  [reduce_gradients(): both = lax.all_gather(mine, 'seq', axis=0, tiled=False)]
    ppermute x0 -> x1, waiting for transfers between devices: none -> 17.5 us  [on_device(): other = lax.ppermute(mine, 'seq', [(0, 1), (1, 0)])]
    dot_general x6, matrix products: 18.3 us -> 4.62 us  [contract_rows(): lax.dot_general(left, right, (((0,), (0,)), ((), ())), preferred_element_...]
    slice x5 -> x8, local copies, waits for them, and re-layouts: 0.97 us -> 13.3 us  [the longest x2 11.5 us: gather_layer(): part = join_columns(packed[:, start:start + size], blocks)]
  transfers between devices with their start and end apart: 19 -> 3, of which waited for: 17 -> 3; matrix products, arithmetic and copies ran while one was open for 9% -> 3% of each run, Pallas kernels for 0% -> 0%
where the time goes in v1:
time: 334 us; the launch traced here: 332 us
  waiting for transfers between devices  191 us (57%)
  local copies, waits for them, and re-layouts  54.3 us (16%)
  matrix products  44.1 us (13%)
  between operations  14.8 us (4%)
  other arithmetic  13.1 us (4%)
  blocking collectives  12.2 us (4%)
    all_gather x1, waiting for transfers between devices, gather_layer(): lax.all_gather(jnp.concatenate(pieces, axis=0), 'fsdp', axis=0, tiled=False)  91.6 us
    reduce_scatter x1, waiting for transfers between devices, reduce_gradients(): mine = lax.psum_scatter(packed, 'fsdp', scatter_dimension=0, tiled=False)  81.6 us
    unnamed x143, local copies, waits for them, and re-layouts  24 us
    ppermute x1, waiting for transfers between devices, on_device(): other = lax.ppermute(mine, 'seq', [(0, 1), (1, 0)])  17.5 us
    all_gather x1, blocking collectives, reduce_gradients(): both = lax.all_gather(mine, 'seq', axis=0, tiled=False)  12.2 us
    slice x2, local copies, waits for them, and re-layouts, gather_layer(): part = join_columns(packed[:, start:start + size], blocks)  11.5 us
    dot_general x6, matrix products, matmul(): return jnp.dot(left, right, preferred_element_type=jnp.float32)  10.9 us
    dot_general x6, matrix products, contract_cols(): lax.dot_general(left, right, (((1,), (1,)), ((), ())), preferred_element_...  9.15 us
  transfers between devices with their start and end apart: 3, of which 3 were waited for; matrix products, arithmetic and copies ran while one was open for 3% of the time, Pallas kernels for 0%

profile of v1, /device:TPU:0, one launch (start us, length us, event | category | flops | bytes accessed | tf_op | source)
XLA Modules:
  0.0 332.5 jit_solution(12957804207004584915)
XLA Ops:
  15.1 5.4 %concatenate.83 = bf16[576]{0:T(1024)(128)(2,1)S(1)} concatenate(bf16[48]{0:T(256)(128)(2,1)} %bitcast.180, bf16[48]{0:T(256)(128)(2,1)} %bitcast.181, bf16[48]{0:T(256)(128)(2,1)} %bitcast.182, bf16[48]{0:T(256)(128)(2,1)} %bitcast.183, bf16[48]{0:T(256)(128)(2,1)} %bitcast.184, bf16[48]{0:T(256)(128)(2,1)} %bitcast.185, bf16[48]{0:T(256)(128)(2,1)} %bitcast.186, ...), dimensions={0} | concatenate | bytes 2304 | tf_op jit(solution)/shard_map/concatenate | solution.py:137
  20.6 1.0 bitcast_dynamic-update-slice_fusion
  22.6 1.0 constant_dynamic-update-slice_fusion.1
  23.7 3.0 collective-permute-start
  26.7 17.5 %collective-permute-done = f32[2,128,768]{2,1,0:T(8,128)S(1)} collective-permute-done((f32[2,128,768]{2,1,0:T(8,128)S(1)}, f32[2,128,768]{2,1,0:T(8,128)S(1)}, u32[]{:S(2)}, u32[]{:S(2)}) %collective-permute-start) | collective-permute-done | bytes 786464 | tf_op jit(solution)/shard_map/ppermute | solution.py:203
  44.4 1.0 fusion.60
  46.4 91.6 %all-gather.3.cloned.1.call-done = bf16[9472,768]{1,0:T(8,128)(2,1)} async-done(((bf16[592,768]{1,0:T(8,128)(2,1)}), bf16[9472,768]{1,0:T(8,128)(2,1)}) %all-gather.3.cloned.1.call-update) | async-done | bytes 14549008 | tf_op jit(solution)/shard_map/all_gather | solution.py:140
  138.0 4.9 %slice.268 = bf16[16,192,768]{2,1,0:T(8,128)(2,1)} slice(bf16[16,592,768]{2,1,0:T(8,128)(2,1)} %bitcast.132), slice={[0:16], [384:576], [0:768]} | slice | bytes 9437184 | tf_op jit(solution)/shard_map/slice | solution.py:146
  142.9 1.0 slice.251
  143.9 6.6 %fusion.65 = (bf16[16,48,768]{2,1,0:T(8,128)(2,1)}, bf16[16,48,768]{2,1,0:T(8,128)(2,1)}, bf16[16,48,768]{2,1,0:T(8,128)(2,1)}, bf16[16,48,768]{2,1,0:T(8,128)(2...) fusion(bf16[16,592,768]{2,1,0:T(8,128)(2,1)} %bitcast.134), kind=kLoop, calls=%fused_computation.157 | loop fusion | bytes 18874368 | tf_op jit(solution)/shard_map/slice | solution.py:146
  154.9 1.9 fusion.25
  159.2 1.7 multiply_reduce_fusion.1
  161.6 1.4 reshape.537
  162.9 1.4 reshape.536
  168.2 3.4 %multiply_convert_fusion.1 = (bf16[256,3072]{1,0:T(8,128)(2,1)}, f32[256,3072]{1,0:T(8,128)S(1)}) fusion(f32[3072]{0:T(1024)S(1)} %copy-done.48, bf16[768,3072]{1,0:T(8,128)(2,1)S(1)} %bitcast.147, f32[256,768]{1,0:T(8,128)S(1)} %get-tuple-element.83, f32[768]{0:T(1024)S(1)} %copy-done.44, f32[768]{0:T(1024)S(1)} %copy-done.36, f32[256]{0:T(256)S(1)} %add_rsqrt_fusion, ...), kind=kOutput, calls=%fused_computation.14 | convolution fusion | flops 1213661184 | bytes 10244096 | tf_op jit(solution)/shard_map/dot_general | solution.py:15
  171.6 3.2 fusion.66
  174.8 2.2 multiply_reduce_fusion.2
  177.1 1.9 add_convert_fusion
  180.7 1.3 convolution_convert_fusion.7
  182.0 1.9 copy.58
  183.9 3.4 %fusion.74 = f32[12,256,256]{1,2,0:T(8,128)} fusion(bf16[256,12,64]{0,2,1:T(8,128)(2,1)} %bitcast.150, bf16[256,12,64]{0,2,1:T(8,128)(2,1)} %bitcast.155), kind=kOutput, calls=%fused_computation.164 | convolution fusion | flops 100663296 | bytes 3932160 | tf_op jit(solution)/shard_map/qhd,khd->hqk/dot_general | solution.py:92
  187.3 5.8 %bitcast_reduce_fusion.1 = (bf16[12,64]{1,0:T(8,128)(2,1)}, bf16[12,64,256]{2,1,0:T(8,128)(2,1)}) fusion(bf16[256,12,64]{0,2,1:T(8,128)(2,1)} %bitcast.167, f32[12,256,256]{1,2,0:T(8,128)} %fusion.74, f32[12,256]{1,0:T(8,128)S(1)} %log_add_fusion, f32[12,256,256]{1,2,0:T(8,128)S(1)} %get-tuple-element.81), kind=kOutput, calls=%fused_computation.78 | convolution fusion | flops 108136960 | bytes 7091712 | tf_op jit(solution)/shard_map/hqk,khd->qhd/dot_general | solution.py:100
  193.1 5.2 %fusion.21 = bf16[12,64,256]{2,1,0:T(8,128)(2,1)} fusion(bf16[256,12,64]{0,2,1:T(8,128)(2,1)} %bitcast.165, f32[12,256,256]{1,2,0:T(8,128)} %fusion.74, f32[12,256]{1,0:T(8,128)S(1)} %log_add_fusion, f32[12,256,256]{1,2,0:T(8,128)S(1)} %get-tuple-element.81), kind=kOutput, calls=%fused_computation.37 | convolution fusion | flops 107941120 | bytes 7090176 | tf_op jit(solution)/shard_map/hqk,qhd->khd/dot_general | solution.py:103
  198.3 2.5 bitcast_reduce_fusion
  204.7 1.0 convolution_convert_fusion.1
  212.0 1.5 fusion.59
  214.5 2.0 convolution_convert_fusion
  216.5 1.7 constant_dynamic-update-slice_fusion.3
  219.9 2.0 fusion.33
  221.9 4.0 %fusion.27 = f32[1,128,768]{2,1,0:T(8,128)} fusion(bf16[3072,768]{1,0:T(8,128)(2,1)} %bitcast.128, bf16[256,3072]{1,0:T(8,128)(2,1)S(1)} %copy-done.7, s32[]{:T(128)S(6)} %select_n.33, f32[256,768]{1,0:T(8,128)S(1)} %copy-done.3, f32[768]{0:T(1024)S(1)} %reshape.539), kind=kOutput, calls=%fused_computation.46 | convolution fusion | flops 604176384 | bytes 6296576 | tf_op jit(solution)/shard_map/dot_general | solution.py:15
  225.9 81.6 %reduce-scatter.2.cloned.1.call-done = bf16[1,592,384]{2,1,0:T(8,128)(2,1)} async-done(((bf16[16,592,384]{2,1,0:T(8,128)(2,1)}), bf16[1,592,384]{2,1,0:T(8,128)(2,1)}) %reduce-scatter.2.cloned.1.call-update) | async-done | bytes 454672 | tf_op jit(solution)/shard_map/reduce_scatter | solution.py:173
  307.5 12.2 %all_gather.11 = bf16[2,592,384]{2,1,0:T(8,128)(2,1)S(1)} all-gather(bf16[1,592,384]{2,1,0:T(8,128)(2,1)} %reduce-scatter.2.cloned.1.call-done), channel_id=1, replica_groups=mesh['seq'=2,'fsdp'=16] {'seq'}, dimensions={0}, use_global_device_ids=true | all-gather | bytes 1363968 | tf_op jit(solution)/shard_map/all_gather | solution.py:174
  (218 shorter events, 41.2 us)
Async XLA Ops:
  7.2 16.5 %copy-start.28 = (f32[1,128,768]{2,1,0:T(8,128)S(1)}, f32[1,128,768]{2,1,0:T(8,128)}, u32[]{:S(2)}) copy-start(f32[1,128,768]{2,1,0:T(8,128)} %param.18) | copy-start | bytes 1179652
  7.2 130.8 %all-gather.3.cloned.1.call-start = ((), (), s32[]{:S(2)}) async-start(), calls=%async_computation.2 | async-start | bytes 15458304 | tf_op jit(solution)/shard_map/all_gather | solution.py:140
  22.6 285.0 %reduce-scatter.2.cloned.1.call-start = ((), (), s32[]{:S(2)}) async-start(), calls=%async_computation.1 | async-start | bytes 7729152 | tf_op jit(solution)/shard_map/reduce_scatter | solution.py:173
  23.7 20.6 %collective-permute-start = (f32[2,128,768]{2,1,0:T(8,128)S(1)}, f32[2,128,768]{2,1,0:T(8,128)S(1)}, u32[]{:S(2)}, u32[]{:S(2)}) collective-permute-start(f32[2,128,768]{2,1,0:T(8,128)S(1)} %constant_dynamic-update-slice_fusion), channel_id=1, source_target_pairs={{0,16},{16,0},{1,17},{17,1},{2,18},{18,2},{3,19},{19,3},{4,20},{20... | collective-permute-start | bytes 2359304 | tf_op jit(solution)/shard_map/ppermute | solution.py:203
  45.4 107.8 %copy-start = (f32[1,256,768]{2,1,0:T(8,128)}, f32[1,256,768]{2,1,0:T(8,128)S(1)}, u32[]{:S(2)}) copy-start(f32[1,256,768]{2,1,0:T(8,128)S(1)} %get-tuple-element.45) | copy-start | bytes 2359300
  46.2 107.1 %copy-start.39 = (f32[256]{0:T(256)}, f32[256]{0:T(256)S(1)}, u32[]{:S(2)}) copy-start(f32[256]{0:T(256)S(1)} %broadcast_multiply_fusion.6) | copy-start | bytes 3076
  46.4 106.8 %copy-start.49 = (f32[256]{0:T(256)}, f32[256]{0:T(256)S(1)}, u32[]{:S(2)}) copy-start(f32[256]{0:T(256)S(1)} %add_rsqrt_fusion.1) | copy-start | bytes 3076
  150.5 6.4 %copy-start.14 = (bf16[16,48,768]{2,1,0:T(8,128)(2,1)}, bf16[16,48,768]{2,1,0:T(8,128)(2,1)S(1)}, u32[]{:S(2)}) copy-start(bf16[16,48,768]{2,1,0:T(8,128)(2,1)S(1)} %get-tuple-element.41) | copy-start | bytes 3538948
  150.5 7.3 %copy-start.4 = (bf16[16,48,768]{2,1,0:T(8,128)(2,1)}, bf16[16,48,768]{2,1,0:T(8,128)(2,1)S(1)}, u32[]{:S(2)}) copy-start(bf16[16,48,768]{2,1,0:T(8,128)(2,1)S(1)} %get-tuple-element.39) | copy-start | bytes 3538948
  154.7 3.1 copy-start.24
  154.9 9.4 %copy-start.20 = (bf16[256,768]{0,1:T(8,128)(2,1)}, bf16[256,768]{0,1:T(8,128)(2,1)S(1)}, u32[]{:S(2)}) copy-start(bf16[256,768]{0,1:T(8,128)(2,1)S(1)} %copy.54) | copy-start | bytes 1179652
  164.3 3.1 copy-start.13
  165.0 3.1 copy-start.18
  166.4 10.6 %copy-start.2 = (f32[256,768]{1,0:T(8,128)}, f32[256,768]{1,0:T(8,128)S(1)}, u32[]{:S(2)}) copy-start(f32[256,768]{1,0:T(8,128)S(1)} %get-tuple-element.83) | copy-start | bytes 2359300
  166.4 10.6 %copy-start.46 = (f32[256]{0:T(256)}, f32[256]{0:T(256)S(1)}, u32[]{:S(2)}) copy-start(f32[256]{0:T(256)S(1)} %broadcast_multiply_fusion.5) | copy-start | bytes 3076
  166.6 10.4 %copy-start.52 = (f32[256]{0:T(256)}, f32[256]{0:T(256)S(1)}, u32[]{:S(2)}) copy-start(f32[256]{0:T(256)S(1)} %add_rsqrt_fusion) | copy-start | bytes 3076
  167.4 4.2 %slice-start = ((s8[4718592]{0:T(1024)(128)(4,1)}), s8[4194304]{0:T(1024)(128)(4,1)S(1)}, s32[]{:S(2)}) async-start(s8[4718592]{0:T(1024)(128)(4,1)} %bitcast.129), calls=%async_computation.3 | async-start | bytes 8388608
  168.2 3.4 %slice-start.1 = ((s8[4718592]{0:T(1024)(128)(4,1)}), s8[524288]{0:T(1024)(128)(4,1)S(1)}, s32[]{:S(2)}) async-start(s8[4718592]{0:T(1024)(128)(4,1)} %bitcast.129), calls=%async_computation.4 | async-start | bytes 1048576
  168.2 3.5 %copy-start.17 = (f32[1,256,768]{2,1,0:T(8,128)S(1)}, f32[1,256,768]{2,1,0:T(8,128)}, u32[]{:S(2)}) copy-start(f32[1,256,768]{2,1,0:T(8,128)} %get-tuple-element.26) | copy-start | bytes 2359300
  198.3 3.1 copy-start.19
  198.3 3.1 copy-start.22
  207.4 4.6 %copy-start.8 = (f32[256,768]{1,0:T(8,128)S(1)}, f32[256,768]{1,0:T(8,128)}, u32[]{:S(2)}) copy-start(f32[256,768]{1,0:T(8,128)} %get-tuple-element.30) | copy-start | bytes 2359300
  207.4 4.6 %copy-start.15 = (bf16[16,48,768]{2,1,0:T(8,128)(2,1)S(1)}, bf16[16,48,768]{2,1,0:T(8,128)(2,1)}, u32[]{:S(2)}) copy-start(bf16[16,48,768]{2,1,0:T(8,128)(2,1)} %copy-done.14) | copy-start | bytes 3538948
  207.4 4.6 %copy-start.33 = (f32[768]{0:T(1024)S(1)}, f32[768]{0:T(1024)}, u32[]{:S(2)}) copy-start(f32[768]{0:T(1024)} %copy-done.31) | copy-start | bytes 9220
  210.1 3.6 %copy-start.56 = (bf16[12,64]{1,0:T(8,128)(2,1)S(1)}, bf16[12,64]{1,0:T(8,128)(2,1)}, u32[]{:S(2)}) copy-start(bf16[12,64]{1,0:T(8,128)(2,1)} %get-tuple-element.88) | copy-start | bytes 4612
  210.1 3.7 %copy-start.42 = (bf16[12,64]{1,0:T(8,128)(2,1)S(1)}, bf16[12,64]{1,0:T(8,128)(2,1)}, u32[]{:S(2)}) copy-start(bf16[12,64]{1,0:T(8,128)(2,1)} %get-tuple-element.90) | copy-start | bytes 4612
  210.1 3.7 %copy-start.54 = (bf16[768]{0:T(1024)(128)(2,1)S(1)}, bf16[768]{0:T(1024)(128)(2,1)}, u32[]{:S(2)}) copy-start(bf16[768]{0:T(1024)(128)(2,1)} %get-tuple-element.92) | copy-start | bytes 4612
  210.1 3.8 %copy-start.58 = (bf16[768]{0:T(1024)(128)(2,1)S(1)}, bf16[768]{0:T(1024)(128)(2,1)}, u32[]{:S(2)}) copy-start(bf16[768]{0:T(1024)(128)(2,1)} %get-tuple-element.17) | copy-start | bytes 4612
  210.1 3.9 %copy-start.57 = (bf16[768]{0:T(1024)(128)(2,1)S(1)}, bf16[768]{0:T(1024)(128)(2,1)}, u32[]{:S(2)}) copy-start(bf16[768]{0:T(1024)(128)(2,1)} %get-tuple-element.20) | copy-start | bytes 4612
  210.2 4.0 %copy-start.55 = (bf16[3072]{0:T(1024)(128)(2,1)S(1)}, bf16[3072]{0:T(1024)(128)(2,1)}, u32[]{:S(2)}) copy-start(bf16[3072]{0:T(1024)(128)(2,1)} %get-tuple-element.42) | copy-start | bytes 18436
  210.2 4.1 %copy-start.43 = (bf16[16,48]{1,0:T(8,128)(2,1)S(1)}, bf16[16,48]{1,0:T(8,128)(2,1)}, u32[]{:S(2)}) copy-start(bf16[16,48]{1,0:T(8,128)(2,1)} %reshape.529) | copy-start | bytes 4612
  211.1 3.4 %copy-start.7 = (bf16[256,3072]{1,0:T(8,128)(2,1)S(1)}, bf16[256,3072]{1,0:T(8,128)(2,1)}, u32[]{:S(2)}) copy-start(bf16[256,3072]{1,0:T(8,128)(2,1)} %get-tuple-element.84) | copy-start | bytes 4718596
  (32 other events, 53.4 us)
Sparse Core Ops, SparseCore 0:
  22.7 115.2 all-gather.2
  219.0 88.4 reduce-scatter.1
